TPU v7x, 32 devices: a whole 2x2x4 slice. The times are simulated.
32 devices in a mesh: dp: 32 (over z, y, x, core).
Axes of the slice: x: 2, y: 2, z: 4, core: 2. Of those that a mesh axis runs over, the one named last changes fastest.
Arguments:
- images: bfloat16 [256, 196, 512], P('dp'), may hold values from -6 to 6
- cotangent: bfloat16 [256, 196, 512], P('dp'), may hold values from -6 to 6
- image_counts: int32 [32], P('dp'), may hold values from 1 to 8, as said below
- shift_mask: int32 [4, 49, 49], replicated, may hold values from 0 to 1, as said below
- rel_index: int32 [49, 49], replicated, may hold values from 0 to 168
- step_count: int32 [1], replicated, may hold values from 1 to 20
- attend_weight: bfloat16 [512, 1536], P('dp'), may hold values from -0.25 to 0.25
- merge_weight: bfloat16 [512, 512], P('dp'), may hold values from -1 to 1
- expand_weight: bfloat16 [512, 2048], P('dp'), may hold values from -0.25 to 0.25
- project_weight: bfloat16 [2048, 512], P('dp'), may hold values from -0.125 to 0.125
- norm_gains: float32 [2, 512], replicated, may hold values from 0.1 to 1.9
- norm_shifts: float32 [2, 512], replicated, may hold values from -2 to 2
- layer_biases: float32 [4608], replicated, may hold values from -2 to 2
- bias_table: float32 [169, 16], replicated, may hold values from -4 to 4
- attend_momentum: float32 [512, 1536], P('dp'), may hold values from -1.2 to 1.2
- merge_momentum: float32 [512, 512], P('dp'), may hold values from -1.2 to 1.2
- expand_momentum: float32 [512, 2048], P('dp'), may hold values from -1.2 to 1.2
- project_momentum: float32 [2048, 512], P('dp'), may hold values from -1.2 to 1.2
- gains_mean: float32 [2, 512], replicated, may hold values from -0.6 to 0.6
- gains_square: float32 [2, 512], replicated, may hold values from 0.0001 to 0.001
- shifts_mean: float32 [2, 512], replicated, may hold values from -0.6 to 0.6
- shifts_square: float32 [2, 512], replicated, may hold values from 0.0001 to 0.001
- biases_mean: float32 [4608], replicated, may hold values from -0.6 to 0.6
- biases_square: float32 [4608], replicated, may hold values from 0.0001 to 0.001
- table_mean: float32 [169, 16], replicated, may hold values from -0.6 to 0.6
- table_square: float32 [169, 16], replicated, may hold values from 0.0001 to 0.001
Outputs:
- block_out: bfloat16 [256, 196, 512], P('dp')
- input_grad: float32 [256, 196, 512], P('dp')
- attend_grad: float32 [512, 1536], P('dp')
- attend_momentum_next: float32 [512, 1536], P('dp')
- attend_update: float32 [512, 1536], P('dp')
- merge_grad: float32 [512, 512], P('dp')
- merge_momentum_next: float32 [512, 512], P('dp')
- merge_update: float32 [512, 512], P('dp')
- expand_grad: float32 [512, 2048], P('dp')
- expand_momentum_next: float32 [512, 2048], P('dp')
- expand_update: float32 [512, 2048], P('dp')
- project_grad: float32 [2048, 512], P('dp')
- project_momentum_next: float32 [2048, 512], P('dp')
- project_update: float32 [2048, 512], P('dp')
- gains_grad: float32 [2, 512], replicated
- gains_mean_next: float32 [2, 512], replicated
- gains_square_next: float32 [2, 512], replicated
- gains_update: float32 [2, 512], replicated
- shifts_grad: float32 [2, 512], replicated
- shifts_mean_next: float32 [2, 512], replicated
- shifts_square_next: float32 [2, 512], replicated
- shifts_update: float32 [2, 512], replicated
- biases_grad: float32 [4608], replicated
- biases_mean_next: float32 [4608], replicated
- biases_square_next: float32 [4608], replicated
- biases_update: float32 [4608], replicated
- table_grad: float32 [169, 16], replicated
- table_mean_next: float32 [169, 16], replicated
- table_square_next: float32 [169, 16], replicated
- table_update: float32 [169, 16], replicated
Inputs may be any that keep to these rules, and one draw needn't show every extreme that they name: `image_counts`: one device holds 8 live images and another holds 1; live images fill a device's first slots. `shift_mask`: 1 where two patches of a window may attend to each other; symmetric, with ones on the diagonal.
All inputs are finite; a program needn't handle non-finite values.
Results may differ from a plain program's by a relative error of at most 0.0095.
The roundings to bfloat16 on the way count: a program that leaves them out, or rounds other values in their place, can miss the bound.
Values may be sent and summed in bfloat16 or wider, within the bound.
No kernel may reach another device: no remote copies, remote signals or barrier semaphores. Data moves between devices by JAX's collectives and lax.ppermute only.
A program may use at most 256 MiB of HBM per device.

v0:
```python
from functools import partial
import math
import jax
import jax.numpy as jnp
from jax import lax
from jax.sharding import PartitionSpec as P

HEADS = 16
WIN = 7
SIDE = 14
SHIFT = 3
WIN_TOK = 49
PATCHES = 196
TABLE = 169
highest = lax.Precision.HIGHEST
newton_first = 3.4445
newton_second = -4.775
newton_third = 2.0315


def as_sent(shard):

    def short(part):
        return part.astype(jnp.bfloat16) if part.dtype == jnp.float32 else part

    return jax.tree.map(short, shard)


def layer_norm(values, gain, shift):
    center = values - jnp.mean(values, axis=-1, keepdims=True)
    spread = jnp.mean(center * center, axis=-1, keepdims=True)
    return center * lax.rsqrt(spread + 1e-05) * gain + shift


def gelu_exact(values):
    return jax.nn.gelu(values, approximate=False)


def to_windows(field):
    count = field.shape[0]
    blocks = SIDE // WIN
    square = field.reshape(count, SIDE, SIDE, field.shape[-1])
    rolled = jnp.roll(square, (-SHIFT, -SHIFT), (1, 2))
    parted = rolled.reshape(count, blocks, WIN, blocks, WIN, field.shape[-1])
    return parted.transpose(0, 1, 3, 2, 4, 5).reshape(
        count * blocks * blocks, WIN * WIN, field.shape[-1]
    )


def from_windows(windows, count):
    blocks = SIDE // WIN
    parted = windows.reshape(count, blocks, blocks, WIN, WIN, windows.shape[-1])
    square = parted.transpose(0, 1, 3, 2, 4, 5).reshape(count, SIDE, SIDE, windows.shape[-1])
    return jnp.roll(square, (SHIFT, SHIFT), (1, 2)).reshape(count, SIDE * SIDE, windows.shape[-1])


def split_heads(rows):
    return rows.reshape(rows.shape[0], rows.shape[1], HEADS, -1).transpose(0, 2, 1, 3)


def merge_heads(rows):
    return rows.transpose(0, 2, 1, 3).reshape(rows.shape[0], rows.shape[2], -1)


def orthogonalize(matrix):
    tall = matrix.shape[0] > matrix.shape[1]
    current = matrix.T if tall else matrix
    current = current / (jnp.sqrt(jnp.sum(current * current)) + 1e-07)
    for sweep in range(5):
        square = jnp.dot(current, current.T, precision=highest)
        mixer = newton_second * square + newton_third * jnp.dot(square, square, precision=highest)
        current = newton_first * current + jnp.dot(mixer, current, precision=highest)
    return current.T if tall else current


def adamw_step(param, grad, first, second, steps):
    first_next = 0.9 * first + 0.1 * grad
    second_next = 0.999 * second + 0.001 * grad * grad
    first_hat = first_next / (1.0 - jnp.power(0.9, steps))
    second_hat = second_next / (1.0 - jnp.power(0.999, steps))
    update = -0.05 * (first_hat / (jnp.sqrt(second_hat) + 1e-08) + 0.05 * param)
    return (first_next, second_next, update)


def padded_rows(flat, length):
    return jnp.pad(flat, ((0, 0), (0, length - flat.shape[1])))


def local(
    images,
    cotangent,
    image_counts,
    shift_mask,
    rel_index,
    step_count,
    attend_weight,
    merge_weight,
    expand_weight,
    project_weight,
    norm_gains,
    norm_shifts,
    layer_biases,
    bias_table,
    attend_momentum,
    merge_momentum,
    expand_momentum,
    project_momentum,
    gains_mean,
    gains_square,
    shifts_mean,
    shifts_square,
    biases_mean,
    biases_square,
    table_mean,
    table_square,
):
    f32 = jnp.float32
    bf16 = jnp.bfloat16
    slots = images.shape[0]
    width = images.shape[2]
    devices = lax.axis_size("dp")
    hidden_units = expand_weight.shape[1]
    scale = 1.0 / math.sqrt(width // HEADS)
    grad_scale = 1.0 / math.sqrt(slots * devices * PATCHES)
    gathered = (
        lax.all_gather(attend_weight, "dp", axis=0, tiled=True),
        lax.all_gather(merge_weight, "dp", axis=0, tiled=True),
        lax.all_gather(expand_weight, "dp", axis=0, tiled=True),
        lax.all_gather(project_weight, "dp", axis=0, tiled=True),
    )
    attend_full, merge_full, expand_full, project_full = gathered
    valid = (jnp.arange(slots) < image_counts[0]).astype(f32)[:, None, None]
    mask_add = -100.0 * (1 - shift_mask).astype(f32)
    masking = jnp.tile(mask_add, (slots, 1, 1))[:, None]
    one_hot = (rel_index.reshape(-1)[:, None] == jnp.arange(TABLE)[None, :]).astype(f32)
    position = jnp.dot(one_hot, bias_table, precision=highest).T.reshape(HEADS, WIN_TOK, WIN_TOK)
    features = images.astype(f32)
    normed, norm_pull = jax.vjp(layer_norm, features, norm_gains[0], norm_shifts[0])
    windows = to_windows(normed.astype(bf16))
    triple = (
        jnp.einsum("wtd,de->wte", windows, attend_full, preferred_element_type=f32)
        + layer_biases[: 3 * width]
    )
    queries = split_heads(triple[..., :width] * scale).astype(bf16)
    keys_low = split_heads(triple[..., width : 2 * width]).astype(bf16)
    values_low = split_heads(triple[..., 2 * width :]).astype(bf16)
    scores = (
        jnp.einsum("whqc,whkc->whqk", queries, keys_low, preferred_element_type=f32)
        + position
        + masking
    )
    attention = jax.nn.softmax(scores, axis=-1)
    attention_low = attention.astype(bf16)
    mixed = merge_heads(
        jnp.einsum("whqk,whkc->whqc", attention_low, values_low, preferred_element_type=f32)
    ).astype(bf16)
    branch = (
        jnp.einsum("wtd,de->wte", mixed, merge_full, preferred_element_type=f32)
        + layer_biases[3 * width : 4 * width]
    )
    middle = features + from_windows(branch, slots)
    normed_two, norm_two_pull = jax.vjp(layer_norm, middle, norm_gains[1], norm_shifts[1])
    normed_low = normed_two.astype(bf16)
    pre_act = (
        jnp.einsum("itd,df->itf", normed_low, expand_full, preferred_element_type=f32)
        + layer_biases[4 * width : 4 * width + hidden_units]
    )
    activated, gelu_pull = jax.vjp(gelu_exact, pre_act)
    active_low = activated.astype(bf16)
    mlp_out = (
        jnp.einsum("itf,fd->itd", active_low, project_full, preferred_element_type=f32)
        + layer_biases[4 * width + hidden_units :]
    )
    block_out = (valid * (middle + mlp_out)).astype(bf16)
    attend_back, merge_back, expand_back, project_back = (
        lax.all_gather(attend_weight, "dp", axis=0, tiled=True),
        lax.all_gather(merge_weight, "dp", axis=0, tiled=True),
        lax.all_gather(expand_weight, "dp", axis=0, tiled=True),
        lax.all_gather(project_weight, "dp", axis=0, tiled=True),
    )
    grad_out = valid * cotangent.astype(f32)
    grad_out_low = grad_out.astype(bf16)
    project_term = jnp.einsum("itf,itd->fd", active_low, grad_out_low, preferred_element_type=f32)
    grad_act = jnp.einsum("itd,fd->itf", grad_out_low, project_back, preferred_element_type=f32)
    grad_pre = gelu_pull(grad_act)[0].astype(bf16)
    expand_term = jnp.einsum("itd,itf->df", normed_low, grad_pre, preferred_element_type=f32)
    grad_normed_two = jnp.einsum("itf,df->itd", grad_pre, expand_back, preferred_element_type=f32)
    grad_mid_norm, gain_two, shift_two = norm_two_pull(grad_normed_two)
    grad_middle = grad_out + grad_mid_norm
    grad_branch = to_windows(grad_middle).astype(bf16)
    merge_term = jnp.einsum("wtd,wte->de", mixed, grad_branch, preferred_element_type=f32)
    grad_mixed = split_heads(
        jnp.einsum("wte,de->wtd", grad_branch, merge_back, preferred_element_type=f32).astype(bf16)
    )
    grad_values = jnp.einsum(
        "whqk,whqc->whkc", attention_low, grad_mixed, preferred_element_type=f32
    )
    grad_attention = jnp.einsum(
        "whqc,whkc->whqk", grad_mixed, values_low, preferred_element_type=f32
    )
    grad_scores = (
        attention * (grad_attention - jnp.sum(grad_attention * attention, axis=-1, keepdims=True))
    ).astype(bf16)
    position_grad = jnp.sum(grad_scores, axis=0, dtype=f32).reshape(HEADS, WIN_TOK * WIN_TOK)
    table_term = jnp.dot(one_hot.T, position_grad.T, precision=highest)
    grad_queries = jnp.einsum("whqk,whkc->whqc", grad_scores, keys_low, preferred_element_type=f32)
    grad_keys = jnp.einsum("whqk,whqc->whkc", grad_scores, queries, preferred_element_type=f32)
    grad_triple = jnp.concatenate(
        [merge_heads(grad_queries) * scale, merge_heads(grad_keys), merge_heads(grad_values)],
        axis=-1,
    ).astype(bf16)
    attend_term = jnp.einsum("wtd,wte->de", windows, grad_triple, preferred_element_type=f32)
    grad_normed = from_windows(
        jnp.einsum("wte,de->wtd", grad_triple, attend_back, preferred_element_type=f32), slots
    )
    grad_feat, gain_one, shift_one = norm_pull(grad_normed)
    input_grad = grad_middle + grad_feat
    bias_term = jnp.concatenate(
        [
            jnp.sum(grad_triple, axis=(0, 1), dtype=f32),
            jnp.sum(grad_branch, axis=(0, 1), dtype=f32),
            jnp.sum(grad_pre, axis=(0, 1), dtype=f32),
            jnp.sum(grad_out_low, axis=(0, 1), dtype=f32),
        ]
    )
    mat_sums = (
        lax.psum_scatter(attend_term, "dp", scatter_dimension=0, tiled=True),
        lax.psum_scatter(merge_term, "dp", scatter_dimension=0, tiled=True),
        lax.psum_scatter(expand_term, "dp", scatter_dimension=0, tiled=True),
        lax.psum_scatter(project_term, "dp", scatter_dimension=0, tiled=True),
    )
    small_sums = lax.psum(
        (jnp.stack([gain_one, gain_two]), jnp.stack([shift_one, shift_two]), bias_term, table_term),
        "dp",
    )
    mat_grads = tuple((term * grad_scale for term in mat_sums))
    small_grads = tuple((term * grad_scale for term in small_sums))
    momenta = (attend_momentum, merge_momentum, expand_momentum, project_momentum)
    momenta_next = tuple((0.95 * moment + grad for moment, grad in zip(momenta, mat_grads)))
    stride = 1
    owner_ranks = [order * stride for order in range(4)]
    rank_index = lax.axis_index("dp")
    shard_sizes = [moment.size for moment in momenta_next]
    longest = max(shard_sizes)
    whole = lax.all_gather(momenta_next, "dp", axis=0, tiled=True)
    owner_terms = tuple(
        (
            lax.cond(
                rank_index == owner_ranks[order],
                partial(orthogonalize, matrix),
                partial(jnp.zeros_like, matrix),
            )
            for order, matrix in enumerate(whole)
        )
    )
    packed = jnp.zeros((devices, longest), f32)
    for order, term in enumerate(owner_terms):
        packed = packed + padded_rows(term.reshape(devices, shard_sizes[order]), longest)
    received = lax.all_to_all(
        as_sent(packed), "dp", split_axis=0, concat_axis=0, tiled=True
    ).astype(packed.dtype)
    orth_rows = tuple(
        (
            received[owner_ranks[order], : shard_sizes[order]].reshape(moment.shape)
            for order, moment in enumerate(momenta_next)
        )
    )
    results = [block_out, input_grad]
    for grad, moment_next, orth_part, matrix in zip(mat_grads, momenta_next, orth_rows, whole):
        update = -0.02 * math.sqrt(max(matrix.shape)) * orth_part
        results += [grad, moment_next, update]
    steps = step_count[0].astype(f32)
    params = (norm_gains, norm_shifts, layer_biases, bias_table)
    states = (
        (gains_mean, gains_square),
        (shifts_mean, shifts_square),
        (biases_mean, biases_square),
        (table_mean, table_square),
    )
    for param, grad, state in zip(params, small_grads, states):
        first_next, second_next, update = adamw_step(param, grad, state[0], state[1], steps)
        results += [grad, first_next, second_next, update]
    return tuple(results)


def solution(mesh):
    return jax.shard_map(
        local,
        mesh=mesh,
        in_specs=(
            P("dp", None, None),
            P("dp", None, None),
            P("dp"),
            P(),
            P(),
            P(),
            P("dp", None),
            P("dp", None),
            P("dp", None),
            P("dp", None),
            P(),
            P(),
            P(),
            P(),
            P("dp", None),
            P("dp", None),
            P("dp", None),
            P("dp", None),
            P(),
            P(),
            P(),
            P(),
            P(),
            P(),
            P(),
            P(),
        ),
        out_specs=(
            P("dp", None, None),
            P("dp", None, None),
            P("dp", None),
            P("dp", None),
            P("dp", None),
            P("dp", None),
            P("dp", None),
            P("dp", None),
            P("dp", None),
            P("dp", None),
            P("dp", None),
            P("dp", None),
            P("dp", None),
            P("dp", None),
            P(),
            P(),
            P(),
            P(),
            P(),
            P(),
            P(),
            P(),
            P(),
            P(),
            P(),
            P(),
            P(),
            P(),
            P(),
            P(),
        ),
        check_vma=False,
    )
```

profile of v0, /device:TPU:0, one launch (start us, length us, event | category | flops | bytes accessed | tf_op | source)
XLA Modules:
  0.0 1322.4 jit_solution(11692982071132868505)
XLA Ops:
  25.4 47.8 %all_gather.41 = bf16[512,512]{1,0:T(8,128)(2,1)} all-gather(bf16[16,512]{1,0:T(8,128)(2,1)S(1)} %copy-done.51), channel_id=1, replica_groups=mesh['dp'=32] {'dp'}, dimensions={0}, use_global_device_ids=true | all-gather | bytes 540672 | tf_op jit(solution)/shard_map/all_gather | solution.py:127
  94.8 11.8 fusion.125
  136.4 9.4 fusion.68
  150.3 31.3 %multiply_convert_fusion.1 = (bf16[8,196,2048]{2,1,0:T(8,128)(2,1)}, f32[8,196,2048]{2,1,0:T(8,128)}) fusion(f32[8,196,2048]{2,1,0:T(8,128)S(1)} %get-tuple-element.268, f32[2048]{0:T(1024)S(1)} %copy-done.46, u8[196,2048]{1,0:T(8,128)(4,1)S(1)} %get-tuple-element.201, u8[196,2048]{1,0:T(8,128)(4,1)S(1)} %get-tuple-element.200), kind=kLoop, calls=%fused_computation.103 | loop fusion | flops 227999744 | bytes 32923648 | tf_op jit(solution)/shard_map/convert_element_type | solution.py:169
  185.8 18.7 %convert_reduce_fusion.1 = (f32[2048]{0:T(1024)}, bf16[8,196,2048]{2,1,0:T(8,128)(2,1)}) fusion(f32[8,196,2048]{2,1,0:T(8,128)} %get-tuple-element.249, bf16[2048,512]{1,0:T(8,128)(2,1)} %all-gather.12.cloned.1.call-done, f32[8]{0:T(128)} %compare_convert_fusion, bf16[8,196,512]{2,0,1:T(8,128)(2,1)} %param.35, f32[8,196,2048]{2,1,0:T(8,128)} %copy-done.10, ...), kind=kOutput, calls=%fused_computation.101 | convolution fusion | flops 3345332224 | bytes 35831840 | tf_op jit(solution)/shard_map/itd,fd->itf/dot_general | solution.py:184
  239.1 10.5 copy.230
  249.6 13.1 multiply_reduce_fusion.4
  262.7 14.6 %convert_reduce_fusion = (f32[16,49,49]{1,2,0:T(8,128)}, bf16[32,16,49,49]{2,3,1,0:T(8,128)(2,1)}) fusion(f32[32,16,49,49]{2,3,1,0:T(8,128)} %get-tuple-element.271, f32[32,16,49]{2,1,0:T(8,128)S(1)} %get-tuple-element.270, f32[32,16,49,49]{2,3,1,0:T(8,128)} %get-tuple-element.267, f32[32,16,49]{2,1,0:T(8,128)S(1)} %get-tuple-element.266), kind=kLoop, calls=%fused_computation.90 | loop fusion | flops 7337456 | bytes 12647488 | tf_op jit(solution)/shard_map/reduce_sum | solution.py:204
  285.8 10.3 convolution_convert_fusion
  345.1 9.3 convolution_bitcast_fusion.1
  354.6 101.1 %reduce-scatter.7.cloned.1.call-done = f32[16,512]{1,0:T(8,128)} async-done(((f32[512,512]{1,0:T(8,128)}), f32[16,512]{1,0:T(8,128)}) %reduce-scatter.7.cloned.1.call-update) | async-done | bytes 32784 | tf_op jit(solution)/shard_map/reduce_scatter | solution.py:228
  457.2 102.7 %reduce-scatter.5.cloned.1.call-done = f32[16,1536]{1,0:T(8,128)} async-done(((f32[512,1536]{1,0:T(8,128)}), f32[16,1536]{1,0:T(8,128)}) %reduce-scatter.5.cloned.1.call-update) | async-done | bytes 98320 | tf_op jit(solution)/shard_map/reduce_scatter | solution.py:227
  561.6 140.6 %reduce-scatter.9.cloned.1.call-done = f32[16,2048]{1,0:T(8,128)} async-done(((f32[512,2048]{1,0:T(8,128)}), f32[16,2048]{1,0:T(8,128)}) %reduce-scatter.9.cloned.1.call-update) | async-done | bytes 131088 | tf_op jit(solution)/shard_map/reduce_scatter | solution.py:229
  704.3 137.2 %reduce-scatter.11.cloned.1.call-done = f32[64,512]{1,0:T(8,128)} async-done(((f32[2048,512]{1,0:T(8,128)}), f32[64,512]{1,0:T(8,128)}) %reduce-scatter.11.cloned.1.call-update) | async-done | bytes 131088 | tf_op jit(solution)/shard_map/reduce_scatter | solution.py:230
  863.6 31.3 %all-gather.16.cloned.1.call-done = f32[512,512]{1,0:T(8,128)} async-done(((f32[16,512]{1,0:T(8,128)}), f32[512,512]{1,0:T(8,128)}) %all-gather.16.cloned.1.call-update) | async-done | bytes 1048592 | tf_op jit(solution)/shard_map/all_gather | solution.py:245
  895.0 11.3 conditional.5
  906.3 50.5 %all-gather.14.cloned.1.call-done = f32[512,1536]{1,0:T(8,128)} async-done(((f32[16,1536]{1,0:T(8,128)}), f32[512,1536]{1,0:T(8,128)}) %all-gather.14.cloned.1.call-update) | async-done | bytes 3145744 | tf_op jit(solution)/shard_map/all_gather | solution.py:245
  956.8 77.7 %conditional.4 = (f32[32,32768]{1,0:T(8,128)}) conditional(s32[]{:T(128)} %convert_element_type.166, () %tuple.40, f32[512,1536]{1,0:T(8,128)} %all-gather.14.cloned.1.call-done), branch_computations={%region_12.13_spmd, %region_13.15_spmd} | conditional | flops 56387174400 | bytes 97517640 | solution.py:248
  1034.5 12.3 conditional.6
  1046.8 39.0 %all-gather.20.cloned.1.call-done = f32[2048,512]{1,0:T(8,128)} async-done(((f32[64,512]{1,0:T(8,128)}), f32[2048,512]{1,0:T(8,128)}) %all-gather.20.cloned.1.call-update) | async-done | bytes 4194320 | tf_op jit(solution)/shard_map/all_gather | solution.py:245
  1108.7 106.6 %all-to-all-start = ((bf16[32,2,16384]{2,1,0:T(2,128)(2,1)}), bf16[32,2,16384]{2,1,0:T(2,128)(2,1)}, u32[]{:S(2)}, u32[]{:S(2)}) async-start(bf16[32,2,16384]{2,1,0:T(2,128)(2,1)} %reshape.321), calls=%async_computation.4 | async-start | bytes 4194304 | tf_op jit(solution)/shard_map/all_to_all | solution.py:259
  1238.1 46.8 %all-reduce.4 = (f32[2,512]{1,0:T(2,128)S(1)}, f32[2,512]{1,0:T(2,128)S(1)}, f32[4608]{0:T(1024)S(1)}, f32[169,16]{0,1:T(8,128)S(1)}) all-reduce(f32[2,512]{1,0:T(2,128)S(1)} %pad_maximum_fusion.9, f32[2,512]{1,0:T(2,128)S(1)} %pad_maximum_fusion.10, f32[4608]{0:T(1024)S(1)} %pad_maximum_fusion.8, ...), channel_id=1, replica_groups=mesh['dp'=32] {'dp'}, use_global_device_ids=true, to_apply=%region_29.30 | all-reduce | flops 9360 | bytes 74880 | tf_op jit(solution)/shard_map/psum | solution.py:232
  1286.9 10.5 reshape.322
  1297.4 11.1 convert_element_type.171
  (318 shorter events, 333.7 us)
Async XLA Ops:
  7.2 67.1 %all-gather.8.cloned.1.call-start = ((), (), s32[]{:S(2)}) async-start(), calls=%async_computation.5 | async-start | bytes 1622016 | tf_op jit(solution)/shard_map/all_gather | solution.py:126
  7.9 128.4 %all-gather.10.cloned.1.call-start = ((), (), s32[]{:S(2)}) async-start(), calls=%async_computation.6 | async-start | bytes 2162688 | tf_op jit(solution)/shard_map/all_gather | solution.py:128
  8.7 177.1 %all-gather.12.cloned.1.call-start = ((), (), s32[]{:S(2)}) async-start(), calls=%async_computation.7 | async-start | bytes 2162688 | tf_op jit(solution)/shard_map/all_gather | solution.py:129
  9.4 446.3 %reduce-scatter.7.cloned.1.call-start = ((), (), s32[]{:S(2)}) async-start(), calls=%async_computation.10 | async-start | bytes 1081344 | tf_op jit(solution)/shard_map/reduce_scatter | solution.py:228
  22.6 58.3 %copy-start.19 = (bf16[32,49,512]{2,0,1:T(8,128)(2,1)}, bf16[32,49,512]{2,0,1:T(8,128)(2,1)S(1)}, u32[]{:S(2)}) copy-start(bf16[32,49,512]{2,0,1:T(8,128)(2,1)S(1)} %reshape.277) | copy-start | bytes 4816900
  134.7 199.9 %copy-start = (f32[8,196,512]{2,1,0:T(8,128)}, f32[8,196,512]{2,1,0:T(8,128)S(1)}, u32[]{:S(2)}) copy-start(f32[8,196,512]{2,1,0:T(8,128)S(1)} %get-tuple-element.251) | copy-start | bytes 9633796
  321.9 238.0 %reduce-scatter.5.cloned.1.call-start = ((), (), s32[]{:S(2)}) async-start(), calls=%async_computation.8 | async-start | bytes 3244032 | tf_op jit(solution)/shard_map/reduce_scatter | solution.py:227
  334.5 367.7 %reduce-scatter.9.cloned.1.call-start = ((), (), s32[]{:S(2)}) async-start(), calls=%async_computation.12 | async-start | bytes 4325376 | tf_op jit(solution)/shard_map/reduce_scatter | solution.py:229
  343.7 497.8 %reduce-scatter.11.cloned.1.call-start = ((), (), s32[]{:S(2)}) async-start(), calls=%async_computation.14 | async-start | bytes 4325376 | tf_op jit(solution)/shard_map/reduce_scatter | solution.py:230
  354.5 101.2 %copy-start.45 = (f32[16,512]{1,0:T(8,128)S(1)}, f32[16,512]{1,0:T(8,128)}, u32[]{:S(2)}) copy-start(f32[16,512]{1,0:T(8,128)} %param.49) | copy-start | bytes 98308
  354.5 205.5 %copy-start.33 = (f32[16,1536]{1,0:T(8,128)S(1)}, f32[16,1536]{1,0:T(8,128)}, u32[]{:S(2)}) copy-start(f32[16,1536]{1,0:T(8,128)} %param.48) | copy-start | bytes 294916
  354.5 347.7 %copy-start.30 = (f32[16,2048]{1,0:T(8,128)S(1)}, f32[16,2048]{1,0:T(8,128)}, u32[]{:S(2)}) copy-start(f32[16,2048]{1,0:T(8,128)} %param.50) | copy-start | bytes 393220
  354.5 487.1 %copy-start.31 = (f32[64,512]{1,0:T(8,128)S(1)}, f32[64,512]{1,0:T(8,128)}, u32[]{:S(2)}) copy-start(f32[64,512]{1,0:T(8,128)} %param.51) | copy-start | bytes 393220
  354.5 489.5 %copy-start.78 = (bf16[512,1536]{1,0:T(8,128)(2,1)S(1)}, bf16[512,1536]{1,0:T(8,128)(2,1)}, u32[]{:S(2)}) copy-start(bf16[512,1536]{1,0:T(8,128)(2,1)} %all-gather.8.cloned.1.call-done) | copy-start | bytes 4718596
  354.5 540.5 %all-gather.16.cloned.1.call-start = ((), (), s32[]{:S(2)}) async-start(), calls=%async_computation.11 | async-start | bytes 1081344 | tf_op jit(solution)/shard_map/all_gather | solution.py:245
  457.1 499.6 %all-gather.14.cloned.1.call-start = ((), (), s32[]{:S(2)}) async-start(), calls=%async_computation.9 | async-start | bytes 3244032 | tf_op jit(solution)/shard_map/all_gather | solution.py:245
  561.5 472.9 %all-gather.18.cloned.1.call-start = ((), (), s32[]{:S(2)}) async-start(), calls=%async_computation.13 | async-start | bytes 4325376 | tf_op jit(solution)/shard_map/all_gather | solution.py:245
  703.8 382.0 %all-gather.20.cloned.1.call-start = ((), (), s32[]{:S(2)}) async-start(), calls=%async_computation.15 | async-start | bytes 4325376 | tf_op jit(solution)/shard_map/all_gather | solution.py:245
  1104.1 111.3 %copy-start.4 = (bf16[8,196,512]{2,0,1:T(8,128)(2,1)S(1)}, bf16[8,196,512]{2,0,1:T(8,128)(2,1)}, u32[]{:S(2)}) copy-start(bf16[8,196,512]{2,0,1:T(8,128)(2,1)} %param.34) | copy-start | bytes 4816900
  1104.1 111.3 %copy-start.26 = (f32[8,196]{1,0:T(8,128)S(1)}, f32[8,196]{1,0:T(8,128)}, u32[]{:S(2)}) copy-start(f32[8,196]{1,0:T(8,128)} %copy-done.25) | copy-start | bytes 18820
  1104.1 111.3 %copy-start.41 = (f32[1,512]{1,0:T(1,128)S(1)}, f32[1,512]{1,0:T(1,128)}, u32[]{:S(2)}) copy-start(f32[1,512]{1,0:T(1,128)} %copy-done.40) | copy-start | bytes 6148
  1108.7 111.4 %copy-start.37 = (f32[8,196]{1,0:T(8,128)S(1)}, f32[8,196]{1,0:T(8,128)}, u32[]{:S(2)}) copy-start(f32[8,196]{1,0:T(8,128)} %copy-done.36) | copy-start | bytes 18820
  1108.7 111.4 %copy-start.29 = (f32[8,196]{1,0:T(8,128)S(1)}, f32[8,196]{1,0:T(8,128)}, u32[]{:S(2)}) copy-start(f32[8,196]{1,0:T(8,128)} %copy-done.28) | copy-start | bytes 18820
  1108.7 178.2 %all-to-all-start = ((bf16[32,2,16384]{2,1,0:T(2,128)(2,1)}), bf16[32,2,16384]{2,1,0:T(2,128)(2,1)}, u32[]{:S(2)}, u32[]{:S(2)}) async-start(bf16[32,2,16384]{2,1,0:T(2,128)(2,1)} %reshape.321), calls=%async_computation.4 | async-start | bytes 4194304 | tf_op jit(solution)/shard_map/all_to_all | solution.py:259
  (67 other events, 1010.1 us)
Sparse Core Ops, SparseCore 0:
  10.9 58.4 all-gather.7
  72.3 55.3 all-gather.9
  130.5 55.2 all-gather.11
  322.0 133.6 reduce-scatter.6
  462.4 97.4 reduce-scatter.4
  562.1 139.9 reduce-scatter.8
  704.5 136.9 reduce-scatter.10
  845.4 49.5 all-gather.15
  898.8 57.8 all-gather.13
  960.4 60.8 all-gather.17
  1025.2 60.5 all-gather.19
where the time goes:
time: 1330 us; the launch traced here: 1320 us
  waiting for transfers between devices  609 us (46%)
  matrix products  214 us (16%)
  local copies, waits for them, and re-layouts  135 us (10%)
  other arithmetic  120 us (9%)
  starting transfers between devices  108 us (8%)
  blocking collectives  94.6 us (7%)
  loops' own time  25.9 us (2%)
  between operations  16.6 us (1%)
    reduce_scatter x1, waiting for transfers between devices, local(): lax.psum_scatter(expand_term, 'dp', scatter_dimension=0, tiled=True)  141 us
    reduce_scatter x1, waiting for transfers between devices, local(): lax.psum_scatter(project_term, 'dp', scatter_dimension=0, tiled=True)  137 us
    all_gather x4, waiting for transfers between devices, local(): whole = lax.all_gather(momenta_next, 'dp', axis=0, tiled=True)  121 us
    all_to_all x1, starting transfers between devices, local(): lax.all_to_all(as_sent(packed), 'dp', split_axis=0, concat_axis=0, tiled=...  107 us
    reduce_scatter x1, waiting for transfers between devices, local(): lax.psum_scatter(attend_term, 'dp', scatter_dimension=0, tiled=True)  103 us
    reduce_scatter x1, waiting for transfers between devices, local(): lax.psum_scatter(merge_term, 'dp', scatter_dimension=0, tiled=True)  101 us
    all_gather x1, blocking collectives, local(): lax.all_gather(merge_weight, 'dp', axis=0, tiled=True)  47.8 us
    psum x1, blocking collectives, local(): lax.psum((jnp.stack([gain_one, gain_two]), jnp.stack([shift_one, shift_tw...  46.8 us
  transfers between devices with their start and end apart: 12, of which 8 were waited for; matrix products, arithmetic and copies ran while one was open for 21% of the time, Pallas kernels for 0%

commit v1 on v0

--- a/solution.py
+++ b/solution.py
@@ -16,6 +16,18 @@
 newton_first = 3.4445
 newton_second = -4.775
 newton_third = 2.0315
+
+
+def gather_by_bits(shard, axis, dim):
+    ways, here, step = (lax.axis_size(axis), lax.axis_index(axis), shard.shape[dim])
+    line, have = (shard, 1)
+    while have < ways:
+        line = jnp.concatenate(
+            [line, lax.ppermute(line, axis, [(d, (d - have) % ways) for d in range(ways)])],
+            axis=dim,
+        )
+        have = 2 * have
+    return jnp.roll(line, here * step, axis=dim)
 
 
 def as_sent(shard):
@@ -124,7 +136,7 @@
     grad_scale = 1.0 / math.sqrt(slots * devices * PATCHES)
     gathered = (
         lax.all_gather(attend_weight, "dp", axis=0, tiled=True),
-        lax.all_gather(merge_weight, "dp", axis=0, tiled=True),
+        gather_by_bits(merge_weight, "dp", 0),
         lax.all_gather(expand_weight, "dp", axis=0, tiled=True),
         lax.all_gather(project_weight, "dp", axis=0, tiled=True),
     )

time: 1330 us -> 1360 us (1.023)
  local copies, waits for them, and re-layouts: 135 us -> 149 us
    unnamed x159 -> x169, local copies, waits for them, and re-layouts: 37 us -> 43.3 us
  transfers between devices with their start and end apart: 12 -> 17, of which waited for: 8 -> 10; matrix products, arithmetic and copies ran while one was open for 21% -> 21% of each run, Pallas kernels for 0% -> 0%
where the time goes in v1:
time: 1360 us; the launch traced here: 1350 us
  waiting for transfers between devices  609 us (45%)
  matrix products  214 us (16%)
  local copies, waits for them, and re-layouts  149 us (11%)
  other arithmetic  121 us (9%)
  starting transfers between devices  116 us (9%)
  blocking collectives  98.9 us (7%)
  loops' own time  25.9 us (2%)
  between operations  16.6 us (1%)
    reduce_scatter x1, waiting for transfers between devices, local(): lax.psum_scatter(expand_term, 'dp', scatter_dimension=0, tiled=True)  140 us
    reduce_scatter x1, waiting for transfers between devices, local(): lax.psum_scatter(project_term, 'dp', scatter_dimension=0, tiled=True)  137 us
    all_gather x4, waiting for transfers between devices, local(): whole = lax.all_gather(momenta_next, 'dp', axis=0, tiled=True)  121 us
    all_to_all x1, starting transfers between devices, local(): lax.all_to_all(as_sent(packed), 'dp', split_axis=0, concat_axis=0, tiled=...  107 us
    reduce_scatter x1, waiting for transfers between devices, local(): lax.psum_scatter(attend_term, 'dp', scatter_dimension=0, tiled=True)  103 us
    reduce_scatter x1, waiting for transfers between devices, local(): lax.psum_scatter(merge_term, 'dp', scatter_dimension=0, tiled=True)  98.1 us
    all_gather x1, blocking collectives, local(): lax.all_gather(merge_weight, 'dp', axis=0, tiled=True)  52.1 us
    psum x1, blocking collectives, local(): lax.psum((jnp.stack([gain_one, gain_two]), jnp.stack([shift_one, shift_tw...  46.8 us
  transfers between devices with their start and end apart: 17, of which 10 were waited for; matrix products, arithmetic and copies ran while one was open for 21% of the time, Pallas kernels for 0%

profile of v1, /device:TPU:0, one launch (start us, length us, event | category | flops | bytes accessed | tf_op | source)
XLA Modules:
  0.0 1350.9 jit_solution(10459665653057383691)
XLA Ops:
  53.7 52.1 %all_gather.42 = bf16[512,512]{1,0:T(8,128)(2,1)} all-gather(bf16[16,512]{1,0:T(8,128)(2,1)S(1)} %copy-done.23), channel_id=1, replica_groups=mesh['dp'=32] {'dp'}, dimensions={0}, use_global_device_ids=true | all-gather | bytes 540672 | tf_op jit(solution)/shard_map/all_gather | solution.py:189
  130.9 11.7 fusion.127
  172.2 9.4 fusion.68
  186.2 31.4 %multiply_convert_fusion.1 = (bf16[8,196,2048]{2,1,0:T(8,128)(2,1)}, f32[8,196,2048]{2,1,0:T(8,128)}) fusion(f32[8,196,2048]{2,1,0:T(8,128)S(1)} %get-tuple-element.278, f32[2048]{0:T(1024)S(1)} %copy-done.47, u8[196,2048]{1,0:T(8,128)(4,1)S(1)} %get-tuple-element.201, u8[196,2048]{1,0:T(8,128)(4,1)S(1)} %get-tuple-element.200), kind=kLoop, calls=%fused_computation.103 | loop fusion | flops 227999744 | bytes 32923648 | tf_op jit(solution)/shard_map/convert_element_type | solution.py:181
  217.6 18.7 %convert_reduce_fusion.1 = (f32[2048]{0:T(1024)}, bf16[8,196,2048]{2,1,0:T(8,128)(2,1)}) fusion(f32[8,196,2048]{2,1,0:T(8,128)} %get-tuple-element.249, bf16[2048,512]{1,0:T(8,128)(2,1)} %all-gather.12.cloned.1.call-done, f32[8]{0:T(128)} %compare_convert_fusion, bf16[8,196,512]{2,0,1:T(8,128)(2,1)} %param.35, f32[8,196,2048]{2,1,0:T(8,128)} %copy-done.10, ...), kind=kOutput, calls=%fused_computation.101 | convolution fusion | flops 3345332224 | bytes 35831840 | tf_op jit(solution)/shard_map/itd,fd->itf/dot_general | solution.py:196
  270.9 10.5 copy.230
  281.4 13.1 multiply_reduce_fusion.4
  294.6 14.6 %convert_reduce_fusion = (f32[16,49,49]{1,2,0:T(8,128)}, bf16[32,16,49,49]{2,3,1,0:T(8,128)(2,1)}) fusion(f32[32,16,49,49]{2,3,1,0:T(8,128)} %get-tuple-element.281, f32[32,16,49]{2,1,0:T(8,128)S(1)} %get-tuple-element.280, f32[32,16,49,49]{2,3,1,0:T(8,128)} %get-tuple-element.277, f32[32,16,49]{2,1,0:T(8,128)S(1)} %get-tuple-element.276), kind=kLoop, calls=%fused_computation.90 | loop fusion | flops 7337456 | bytes 12647488 | tf_op jit(solution)/shard_map/reduce_sum | solution.py:216
  317.6 10.3 convolution_convert_fusion
  377.0 9.3 convolution_bitcast_fusion.1
  386.4 98.1 %reduce-scatter.7.cloned.1.call-done = f32[16,512]{1,0:T(8,128)} async-done(((f32[512,512]{1,0:T(8,128)}), f32[16,512]{1,0:T(8,128)}) %reduce-scatter.7.cloned.1.call-update) | async-done | bytes 32784 | tf_op jit(solution)/shard_map/reduce_scatter | solution.py:240
  486.0 102.8 %reduce-scatter.5.cloned.1.call-done = f32[16,1536]{1,0:T(8,128)} async-done(((f32[512,1536]{1,0:T(8,128)}), f32[16,1536]{1,0:T(8,128)}) %reduce-scatter.5.cloned.1.call-update) | async-done | bytes 98320 | tf_op jit(solution)/shard_map/reduce_scatter | solution.py:239
  590.4 140.5 %reduce-scatter.9.cloned.1.call-done = f32[16,2048]{1,0:T(8,128)} async-done(((f32[512,2048]{1,0:T(8,128)}), f32[16,2048]{1,0:T(8,128)}) %reduce-scatter.9.cloned.1.call-update) | async-done | bytes 131088 | tf_op jit(solution)/shard_map/reduce_scatter | solution.py:241
  733.1 137.0 %reduce-scatter.11.cloned.1.call-done = f32[64,512]{1,0:T(8,128)} async-done(((f32[2048,512]{1,0:T(8,128)}), f32[64,512]{1,0:T(8,128)}) %reduce-scatter.11.cloned.1.call-update) | async-done | bytes 131088 | tf_op jit(solution)/shard_map/reduce_scatter | solution.py:242
  892.2 31.3 %all-gather.16.cloned.1.call-done = f32[512,512]{1,0:T(8,128)} async-done(((f32[16,512]{1,0:T(8,128)}), f32[512,512]{1,0:T(8,128)}) %all-gather.16.cloned.1.call-update) | async-done | bytes 1048592 | tf_op jit(solution)/shard_map/all_gather | solution.py:257
  923.4 11.3 conditional.5
  934.7 50.5 %all-gather.14.cloned.1.call-done = f32[512,1536]{1,0:T(8,128)} async-done(((f32[16,1536]{1,0:T(8,128)}), f32[512,1536]{1,0:T(8,128)}) %all-gather.14.cloned.1.call-update) | async-done | bytes 3145744 | tf_op jit(solution)/shard_map/all_gather | solution.py:257
  985.2 77.7 %conditional.4 = (f32[32,32768]{1,0:T(8,128)}) conditional(s32[]{:T(128)} %convert_element_type.166, () %tuple.40, f32[512,1536]{1,0:T(8,128)} %all-gather.14.cloned.1.call-done), branch_computations={%region_12.13_spmd, %region_13.15_spmd} | conditional | flops 56387174400 | bytes 97517640 | solution.py:260
  1062.9 12.3 conditional.6
  1075.2 39.0 %all-gather.20.cloned.1.call-done = f32[2048,512]{1,0:T(8,128)} async-done(((f32[64,512]{1,0:T(8,128)}), f32[2048,512]{1,0:T(8,128)}) %all-gather.20.cloned.1.call-update) | async-done | bytes 4194320 | tf_op jit(solution)/shard_map/all_gather | solution.py:257
  1137.2 106.8 %all-to-all-start = ((bf16[32,2,16384]{2,1,0:T(2,128)(2,1)}), bf16[32,2,16384]{2,1,0:T(2,128)(2,1)}, u32[]{:S(2)}, u32[]{:S(2)}) async-start(bf16[32,2,16384]{2,1,0:T(2,128)(2,1)} %reshape.322), calls=%async_computation.4 | async-start | bytes 4194304 | tf_op jit(solution)/shard_map/all_to_all | solution.py:271
  1266.6 46.8 %all-reduce.4 = (f32[2,512]{1,0:T(2,128)S(1)}, f32[2,512]{1,0:T(2,128)S(1)}, f32[4608]{0:T(1024)S(1)}, f32[169,16]{0,1:T(8,128)S(1)}) all-reduce(f32[2,512]{1,0:T(2,128)S(1)} %pad_maximum_fusion.12, f32[2,512]{1,0:T(2,128)S(1)} %pad_maximum_fusion.13, f32[4608]{0:T(1024)S(1)} %pad_maximum_fusion.11, ...), channel_id=1, replica_groups=mesh['dp'=32] {'dp'}, use_global_device_ids=true, to_apply=%region_29.30 | all-reduce | flops 9360 | bytes 74880 | tf_op jit(solution)/shard_map/psum | solution.py:244
  1315.5 10.4 reshape.323
  1325.9 11.1 convert_element_type.171
  (343 shorter events, 361.2 us)
Async XLA Ops:
  7.2 103.2 %all-gather.8.cloned.1.call-start = ((), (), s32[]{:S(2)}) async-start(), calls=%async_computation.5 | async-start | bytes 1622016 | tf_op jit(solution)/shard_map/all_gather | solution.py:138
  7.9 164.2 %all-gather.10.cloned.1.call-start = ((), (), s32[]{:S(2)}) async-start(), calls=%async_computation.6 | async-start | bytes 2162688 | tf_op jit(solution)/shard_map/all_gather | solution.py:140
  8.7 208.8 %all-gather.12.cloned.1.call-start = ((), (), s32[]{:S(2)}) async-start(), calls=%async_computation.7 | async-start | bytes 2162688 | tf_op jit(solution)/shard_map/all_gather | solution.py:141
  8.7 19.4 %collective-permute-start = (bf16[16,512]{1,0:T(8,128)(2,1)}, bf16[16,512]{1,0:T(8,128)(2,1)S(1)}, u32[]{:S(2)}, u32[]{:S(2)}) collective-permute-start(bf16[16,512]{1,0:T(8,128)(2,1)} %param.41), channel_id=1, source_target_pairs={{0,31},{1,0},{2,1},{3,2},{4,3},{5,4},{6,5},{7,6},{8,7},{9,8},{10,9... | collective-permute-start | bytes 49160 | tf_op jit(solution)/shard_map/ppermute | solution.py:26
  15.2 469.3 %reduce-scatter.7.cloned.1.call-start = ((), (), s32[]{:S(2)}) async-start(), calls=%async_computation.10 | async-start | bytes 1081344 | tf_op jit(solution)/shard_map/reduce_scatter | solution.py:240
  28.2 4.0 collective-permute-start.1
  32.2 4.3 collective-permute-start.2
  36.5 5.6 collective-permute-start.3
  42.8 63.1 %collective-permute-start.4 = (bf16[256,512]{1,0:T(8,128)(2,1)}, bf16[256,512]{1,0:T(8,128)(2,1)S(1)}, u32[]{:S(2)}, u32[]{:S(2)}) collective-permute-start(bf16[256,512]{1,0:T(8,128)(2,1)} %get-tuple-element.258), channel_id=1, source_target_pairs={{0,16},{1,17},{2,18},{3,19},{4,20},{5,21},{6,22},{7,23},{8,24},{9,... | collective-permute-start | bytes 786440 | tf_op jit(solution)/shard_map/ppermute | solution.py:26
  170.5 195.9 %copy-start = (f32[8,196,512]{2,1,0:T(8,128)}, f32[8,196,512]{2,1,0:T(8,128)S(1)}, u32[]{:S(2)}) copy-start(f32[8,196,512]{2,1,0:T(8,128)S(1)} %get-tuple-element.251) | copy-start | bytes 9633796
  353.8 235.0 %reduce-scatter.5.cloned.1.call-start = ((), (), s32[]{:S(2)}) async-start(), calls=%async_computation.8 | async-start | bytes 3244032 | tf_op jit(solution)/shard_map/reduce_scatter | solution.py:239
  366.4 364.5 %reduce-scatter.9.cloned.1.call-start = ((), (), s32[]{:S(2)}) async-start(), calls=%async_computation.12 | async-start | bytes 4325376 | tf_op jit(solution)/shard_map/reduce_scatter | solution.py:241
  375.6 494.5 %reduce-scatter.11.cloned.1.call-start = ((), (), s32[]{:S(2)}) async-start(), calls=%async_computation.14 | async-start | bytes 4325376 | tf_op jit(solution)/shard_map/reduce_scatter | solution.py:242
  386.3 202.5 %copy-start.34 = (f32[16,1536]{1,0:T(8,128)S(1)}, f32[16,1536]{1,0:T(8,128)}, u32[]{:S(2)}) copy-start(f32[16,1536]{1,0:T(8,128)} %param.48) | copy-start | bytes 294916
  386.3 344.6 %copy-start.31 = (f32[16,2048]{1,0:T(8,128)S(1)}, f32[16,2048]{1,0:T(8,128)}, u32[]{:S(2)}) copy-start(f32[16,2048]{1,0:T(8,128)} %param.50) | copy-start | bytes 393220
  386.3 483.7 %copy-start.32 = (f32[64,512]{1,0:T(8,128)S(1)}, f32[64,512]{1,0:T(8,128)}, u32[]{:S(2)}) copy-start(f32[64,512]{1,0:T(8,128)} %param.51) | copy-start | bytes 393220
  386.3 486.1 %copy-start.78 = (bf16[512,1536]{1,0:T(8,128)(2,1)S(1)}, bf16[512,1536]{1,0:T(8,128)(2,1)}, u32[]{:S(2)}) copy-start(bf16[512,1536]{1,0:T(8,128)(2,1)} %all-gather.8.cloned.1.call-done) | copy-start | bytes 4718596
  386.4 537.1 %all-gather.16.cloned.1.call-start = ((), (), s32[]{:S(2)}) async-start(), calls=%async_computation.11 | async-start | bytes 1081344 | tf_op jit(solution)/shard_map/all_gather | solution.py:257
  485.9 499.3 %all-gather.14.cloned.1.call-start = ((), (), s32[]{:S(2)}) async-start(), calls=%async_computation.9 | async-start | bytes 3244032 | tf_op jit(solution)/shard_map/all_gather | solution.py:257
  590.4 472.5 %all-gather.18.cloned.1.call-start = ((), (), s32[]{:S(2)}) async-start(), calls=%async_computation.13 | async-start | bytes 4325376 | tf_op jit(solution)/shard_map/all_gather | solution.py:257
  732.6 381.7 %all-gather.20.cloned.1.call-start = ((), (), s32[]{:S(2)}) async-start(), calls=%async_computation.15 | async-start | bytes 4325376 | tf_op jit(solution)/shard_map/all_gather | solution.py:257
  1137.2 111.5 %copy-start.38 = (f32[8,196]{1,0:T(8,128)S(1)}, f32[8,196]{1,0:T(8,128)}, u32[]{:S(2)}) copy-start(f32[8,196]{1,0:T(8,128)} %copy-done.37) | copy-start | bytes 18820
  1137.2 111.6 %copy-start.30 = (f32[8,196]{1,0:T(8,128)S(1)}, f32[8,196]{1,0:T(8,128)}, u32[]{:S(2)}) copy-start(f32[8,196]{1,0:T(8,128)} %copy-done.29) | copy-start | bytes 18820
  1137.2 178.3 %all-to-all-start = ((bf16[32,2,16384]{2,1,0:T(2,128)(2,1)}), bf16[32,2,16384]{2,1,0:T(2,128)(2,1)}, u32[]{:S(2)}, u32[]{:S(2)}) async-start(bf16[32,2,16384]{2,1,0:T(2,128)(2,1)} %reshape.322), calls=%async_computation.4 | async-start | bytes 4194304 | tf_op jit(solution)/shard_map/all_to_all | solution.py:271
  (72 other events, 1523.0 us)
Sparse Core Ops, SparseCore 0:
  10.9 60.1 all-gather.7
  74.0 55.5 all-gather.9
  132.4 55.2 all-gather.11
  353.9 130.6 reduce-scatter.6
  491.3 97.4 reduce-scatter.4
  591.0 139.8 reduce-scatter.8
  733.3 136.7 reduce-scatter.10
  873.9 49.5 all-gather.15
  927.3 57.8 all-gather.13
  988.9 60.8 all-gather.17
  1053.6 60.5 all-gather.19
